TPU v7x, 32 devices: a whole 2x2x4 slice. The times are simulated.
32 devices in a mesh: dp: 4 (over z), mp: 8 (over y, x, core).
Axes of the slice: x: 2, y: 2, z: 4, core: 2. Of those that a mesh axis runs over, the one named last changes fastest.
Arguments:
- behaviors: bfloat16 [32, 2048, 1024], P('dp', 'mp'), may hold values from -8 to 8
- candidates: bfloat16 [32, 2048, 128], P('dp', 'mp'), may hold values from -12 to 12
- lengths: int32 [32], P('dp'), may hold values from 128 to 1024
- bilinear: bfloat16 [2048, 2048], P('mp'), may hold values from -1 to 2
- norm_gain: float32 [2048], replicated, may hold values from 0.1 to 1.9
- w_gate: bfloat16 [2048, 8192], P('dp', 'mp'), may hold values from -0.125 to 0.125
- w_up: bfloat16 [2048, 8192], P('dp', 'mp'), may hold values from -0.125 to 0.125
- w_down: bfloat16 [8192, 2048], P('mp', 'dp'), may hold values from -0.0625 to 0.0625
Outputs:
- interest: bfloat16 [32, 2048, 128], P('dp', 'mp')
All inputs are finite; a program needn't handle non-finite values.
Results may differ from a plain program's by a relative error of at most 0.015.
Values may be sent and summed in bfloat16 or wider, within the bound.
No kernel may reach another device: no remote copies, remote signals or barrier semaphores. Data moves between devices by JAX's collectives and lax.ppermute only.
A program may use at most 64 MiB of HBM per device.

v0:
```python
import math
import jax
import jax.numpy as jnp
from jax import lax
from jax.sharding import PartitionSpec as P


def attention_weights(scores, live):
    masked = jnp.where(live, scores, -1e30)
    highest = jnp.max(masked, axis=-1, keepdims=True)
    expons = jnp.where(live, jnp.exp(masked - highest), 0.0)
    return (expons / jnp.sum(expons, axis=-1, keepdims=True)).astype(jnp.bfloat16)


def shards(behaviors, candidates, lengths, bilinear, norm_gain, w_gate, w_up, w_down):
    user_count, width_part, cand_count = candidates.shape
    feature_width = bilinear.shape[1]
    behavior_count = behaviors.shape[2]
    query_part = jnp.einsum(
        "ek,ukc->uec",
        bilinear,
        lax.all_gather(candidates, "mp", axis=1, tiled=True),
        preferred_element_type=jnp.float32,
    )
    query = query_part.astype(jnp.bfloat16)
    partial_value = jnp.einsum("ukc,ukl->ucl", query, behaviors, preferred_element_type=jnp.float32)
    scale = 1.0 / math.sqrt(feature_width)
    live = (
        lax.broadcasted_iota(jnp.int32, (user_count, 1, behavior_count), 2) < lengths[:, None, None]
    )
    share = lax.psum_scatter(partial_value, "mp", scatter_dimension=1, tiled=True)
    probs_share = attention_weights(share * scale, live)
    probs = lax.all_gather(probs_share, "mp", axis=1, tiled=True)
    pooled = jnp.einsum(
        "ucl,ukl->ukc", probs, behaviors, preferred_element_type=jnp.float32
    ).astype(jnp.bfloat16)
    whole = lax.all_gather(pooled, "mp", axis=1, tiled=True)
    values = whole.astype(jnp.float32)
    square_mean = jnp.mean(values * values, axis=1, keepdims=True)
    normed = (values * lax.rsqrt(square_mean + 1e-06) * norm_gain[None, :, None]).astype(
        jnp.bfloat16
    )
    gate = jnp.einsum(
        "ukc,kf->ucf",
        normed,
        lax.all_gather(w_gate, "dp", axis=0, tiled=True),
        preferred_element_type=jnp.float32,
    )
    upward = jnp.einsum(
        "ukc,kf->ucf",
        normed,
        lax.all_gather(w_up, "dp", axis=0, tiled=True),
        preferred_element_type=jnp.float32,
    )
    hidden = (jax.nn.silu(gate) * upward).astype(jnp.bfloat16)
    down_full = lax.all_gather(w_down, "dp", axis=1, tiled=True)
    result = lax.psum_scatter(
        jnp.einsum("ucf,fk->kuc", hidden, down_full, preferred_element_type=jnp.float32).astype(
            jnp.bfloat16
        ),
        "mp",
        scatter_dimension=0,
        tiled=True,
    ).astype(jnp.float32)
    return jnp.transpose(result, (1, 0, 2)).astype(jnp.bfloat16)


def solution(mesh):
    return jax.shard_map(
        shards,
        mesh=mesh,
        in_specs=(
            P("dp", "mp", None),
            P("dp", "mp", None),
            P("dp"),
            P("mp", None),
            P(),
            P("dp", "mp"),
            P("dp", "mp"),
            P("mp", "dp"),
        ),
        out_specs=P("dp", "mp", None),
        check_vma=False,
    )
```

profile of v0, /device:TPU:0, one launch (start us, length us, event | category | flops | bytes accessed | tf_op | source)
XLA Modules:
  0.0 498.7 jit_solution(1023455317639719504)
XLA Ops:
  6.5 0.7 all-gather.7.cloned.1.call-update
  7.3 41.3 %all-gather.7.cloned.1.call-done = bf16[8,2048,128]{2,1,0:T(8,128)(2,1)} async-done(((bf16[8,256,128]{2,1,0:T(8,128)(2,1)}), bf16[8,2048,128]{2,1,0:T(8,128)(2,1)}) %all-gather.7.cloned.1.call-update) | async-done | bytes 4194320 | tf_op jit(solution)/shard_map/all_gather | solution.py:22
  48.6 8.2 %fusion.24 = f32[8,128,1024]{2,1,0:T(8,128)} fusion(bf16[8,256,1024]{2,1,0:T(8,128)(2,1)} %param.8, bf16[8,2048,128]{2,1,0:T(8,128)(2,1)} %all-gather.7.cloned.1.call-done, bf16[256,2048]{1,0:T(8,128)(2,1)S(1)} %copy-done), kind=kOutput, calls=%fused_computation.18 | convolution fusion | flops 1610874880 | bytes 13631488 | tf_op jit(solution)/shard_map/ukc,ukl->ucl/dot_general | solution.py:26
  56.8 0.0 all-gather.9.cloned.1.call-start
  56.8 0.6 copy-done.1
  57.4 0.1 iota_compare_fusion
  57.5 50.5 %reduce-scatter.3.cloned.1.call-done = f32[8,16,1024]{2,1,0:T(8,128)} async-done(((f32[8,128,1024]{2,1,0:T(8,128)}), f32[8,16,1024]{2,1,0:T(8,128)}) %reduce-scatter.3.cloned.1.call-update) | async-done | bytes 524304 | tf_op jit(solution)/shard_map/reduce_scatter | solution.py:31
  108.0 1.7 fusion.37
  109.7 0.8 divide_convert_fusion
  110.6 27.9 %all-gather.9.cloned.1.call-done = bf16[8,128,1024]{2,1,0:T(8,128)(2,1)} async-done(((bf16[8,16,1024]{2,1,0:T(8,128)(2,1)}), bf16[8,128,1024]{2,1,0:T(8,128)(2,1)}) %all-gather.9.cloned.1.call-update) | async-done | bytes 2097168 | tf_op jit(solution)/shard_map/all_gather | solution.py:33
  138.5 5.2 %fusion.27 = bf16[8,256,128]{1,2,0:T(8,128)(2,1)} fusion(bf16[8,128,1024]{2,1,0:T(8,128)(2,1)} %all-gather.9.cloned.1.call-done, bf16[8,256,1024]{2,1,0:T(8,128)(2,1)} %param.8), kind=kOutput, calls=%fused_computation.21 | convolution fusion | flops 537133056 | bytes 6815744 | tf_op jit(solution)/shard_map/ucl,ukl->ukc/dot_general | solution.py:34
  143.7 0.5 all-gather.13.cloned.1.call-update
  144.3 0.5 all-gather.15.cloned.1.call-update
  144.9 0.7 all-gather.17.cloned.1.call-update
  145.6 0.2 reduce-scatter.5.cloned.1.call-start
  145.8 35.4 %all-gather.11.cloned.1.call-done = bf16[8,2048,128]{1,2,0:T(8,128)(2,1)} async-done(((bf16[8,256,128]{1,2,0:T(8,128)(2,1)}), bf16[8,2048,128]{1,2,0:T(8,128)(2,1)}) %all-gather.11.cloned.1.call-update) | async-done | bytes 4194320 | tf_op jit(solution)/shard_map/all_gather | solution.py:37
  181.2 3.1 fusion.1
  184.3 79.1 %all-gather.13.cloned.1.call-done = bf16[2048,1024]{1,0:T(8,128)(2,1)} async-done(((bf16[512,1024]{1,0:T(8,128)(2,1)}), bf16[2048,1024]{1,0:T(8,128)(2,1)}) %all-gather.13.cloned.1.call-update) | async-done | bytes 4194320 | tf_op jit(solution)/shard_map/all_gather | solution.py:46
  263.4 9.9 %fusion.8 = f32[8,128,1024]{2,1,0:T(8,128)} fusion(bf16[2048,1024]{1,0:T(8,128)(2,1)} %all-gather.13.cloned.1.call-done, bf16[8,2048,128]{1,2,0:T(8,128)(2,1)} %all-gather.11.cloned.1.call-done, f32[2048]{0:T(1024)S(1)} %copy-done.2, f32[8,128]{1,0:T(8,128)S(1)} %add_rsqrt_fusion), kind=kOutput, calls=%fused_computation.10 | convolution fusion | flops 4303355904 | bytes 12595200 | tf_op jit(solution)/shard_map/ukc,kf->ucf/dot_general | solution.py:43
  273.3 70.7 %all-gather.15.cloned.1.call-done = bf16[2048,1024]{1,0:T(8,128)(2,1)} async-done(((bf16[512,1024]{1,0:T(8,128)(2,1)}), bf16[2048,1024]{1,0:T(8,128)(2,1)}) %all-gather.15.cloned.1.call-update) | async-done | bytes 4194320 | tf_op jit(solution)/shard_map/all_gather | solution.py:52
  344.0 80.8 %all-gather.17.cloned.1.call-done = bf16[1024,2048]{1,0:T(8,128)(2,1)} async-done(((bf16[1024,512]{1,0:T(8,128)(2,1)}), bf16[1024,2048]{1,0:T(8,128)(2,1)}) %all-gather.17.cloned.1.call-update) | async-done | bytes 4194320 | tf_op jit(solution)/shard_map/all_gather | solution.py:56
  424.9 15.2 %convert_bitcast_fusion = bf16[2048,8,128]{0,2,1:T(8,128)(2,1)} fusion(bf16[1024,2048]{1,0:T(8,128)(2,1)} %all-gather.17.cloned.1.call-done, f32[8,128,1024]{2,1,0:T(8,128)} %fusion.8, bf16[2048,1024]{1,0:T(8,128)(2,1)} %all-gather.15.cloned.1.call-done, bf16[8,2048,128]{1,2,0:T(8,128)(2,1)} %all-gather.11.cloned.1.call-done, f32[2048]{0:T(1024)S(1)} %copy-done.2, ...), kind=kOutput, calls=%fused_computation.12 | convolution fusion | flops 8606711808 | bytes 20983808 | tf_op jit(solution)/shard_map/ucf,fk->kuc/dot_general | solution.py:58
  440.1 49.7 %reduce-scatter.5.cloned.1.call-done = bf16[256,8,128]{0,2,1:T(8,128)(2,1)} async-done(((bf16[2048,8,128]{0,2,1:T(8,128)(2,1)}), bf16[256,8,128]{0,2,1:T(8,128)(2,1)}) %reduce-scatter.5.cloned.1.call-update) | async-done | bytes 524304 | tf_op jit(solution)/shard_map/reduce_scatter | solution.py:57
  489.8 2.0 copy.9
  (16 shorter events, 0.3 us)
Async XLA Ops:
  6.5 42.0 %copy-start = (bf16[256,2048]{1,0:T(8,128)(2,1)S(1)}, bf16[256,2048]{1,0:T(8,128)(2,1)}, u32[]{:S(2)}) copy-start(bf16[256,2048]{1,0:T(8,128)(2,1)} %param.11) | copy-start | bytes 3145732
  6.5 42.0 %all-gather.7.cloned.1.call-start = ((), (), s32[]{:S(2)}) async-start(), calls=%async_computation.2 | async-start | bytes 4718592 | tf_op jit(solution)/shard_map/all_gather | solution.py:22
  7.3 100.8 %reduce-scatter.3.cloned.1.call-start = ((), (), s32[]{:S(2)}) async-start(), calls=%async_computation.3 | async-start | bytes 4718592 | tf_op jit(solution)/shard_map/reduce_scatter | solution.py:31
  56.7 0.7 copy-start.1
  56.8 81.7 %all-gather.9.cloned.1.call-start = ((), (), s32[]{:S(2)}) async-start(), calls=%async_computation.4 | async-start | bytes 2359296 | tf_op jit(solution)/shard_map/all_gather | solution.py:33
  110.6 70.6 %all-gather.11.cloned.1.call-start = ((), (), s32[]{:S(2)}) async-start(), calls=%async_computation.5 | async-start | bytes 4718592 | tf_op jit(solution)/shard_map/all_gather | solution.py:37
  143.7 119.7 %copy-start.2 = (f32[2048]{0:T(1024)S(1)}, f32[2048]{0:T(1024)}, u32[]{:S(2)}) copy-start(f32[2048]{0:T(1024)} %param.12) | copy-start | bytes 24580
  143.7 119.7 %all-gather.13.cloned.1.call-start = ((), (), s32[]{:S(2)}) async-start(), calls=%async_computation.6 | async-start | bytes 5242880 | tf_op jit(solution)/shard_map/all_gather | solution.py:46
  144.3 199.8 %all-gather.15.cloned.1.call-start = ((), (), s32[]{:S(2)}) async-start(), calls=%async_computation.7 | async-start | bytes 5242880 | tf_op jit(solution)/shard_map/all_gather | solution.py:52
  144.8 280.0 %all-gather.17.cloned.1.call-start = ((), (), s32[]{:S(2)}) async-start(), calls=%async_computation.8 | async-start | bytes 5242880 | tf_op jit(solution)/shard_map/all_gather | solution.py:56
  145.6 344.2 %reduce-scatter.5.cloned.1.call-start = ((), (), s32[]{:S(2)}) async-start(), calls=%async_computation.9 | async-start | bytes 4718592 | tf_op jit(solution)/shard_map/reduce_scatter | solution.py:57
Sparse Core Ops, SparseCore 0:
  9.2 39.2 all-gather.6
  56.9 51.0 reduce-scatter.2
  110.7 27.7 all-gather.8
  143.8 37.3 all-gather.10
  182.6 80.7 all-gather.12
  264.8 79.2 all-gather.14
  345.6 79.2 all-gather.16
  440.2 49.5 reduce-scatter.4
where the time goes:
time: 499 us
  waiting for transfers between devices  438 us (88%)
  matrix products  38.4 us (8%)
  between operations  13.5 us (3%)
  other arithmetic  5.68 us (1%)
    all_gather x1, waiting for transfers between devices, shards(): down_full = lax.all_gather(w_down, 'dp', axis=1, tiled=True)  80.8 us
    all_gather x1, waiting for transfers between devices, shards(): lax.all_gather(w_gate, 'dp', axis=0, tiled=True)  79.1 us
    all_gather x1, waiting for transfers between devices, shards(): lax.all_gather(w_up, 'dp', axis=0, tiled=True)  70.7 us
    reduce_scatter x1, waiting for transfers between devices, shards(): lax.psum_scatter(partial_value, 'mp', scatter_dimension=1, tiled=True)  50.5 us
    reduce_scatter x1, waiting for transfers between devices, shards(): lax.psum_scatter(jnp.einsum('ucf,fk->kuc', hidden, down_full, preferred_e...  49.7 us
    all_gather x1, waiting for transfers between devices, shards(): lax.all_gather(candidates, 'mp', axis=1, tiled=True)  41.3 us
    all_gather x1, waiting for transfers between devices, shards(): whole = lax.all_gather(pooled, 'mp', axis=1, tiled=True)  35.4 us
    all_gather x1, waiting for transfers between devices, shards(): probs = lax.all_gather(probs_share, 'mp', axis=1, tiled=True)  27.9 us
  transfers between devices with their start and end apart: 8, of which 8 were waited for; matrix products, arithmetic and copies ran while one was open for 3% of the time, Pallas kernels for 0%

commit v1 on v0

--- a/solution.py
+++ b/solution.py
@@ -3,6 +3,11 @@
 import jax.numpy as jnp
 from jax import lax
 from jax.sharding import PartitionSpec as P
+
+
+def gathered_along(value, mesh_axis, along):
+    blocks = lax.all_gather(value, mesh_axis)
+    return jnp.concatenate(blocks, axis=along)
 
 
 def attention_weights(scores, live):
@@ -34,7 +39,7 @@
     pooled = jnp.einsum(
         "ucl,ukl->ukc", probs, behaviors, preferred_element_type=jnp.float32
     ).astype(jnp.bfloat16)
-    whole = lax.all_gather(pooled, "mp", axis=1, tiled=True)
+    whole = gathered_along(pooled, "mp", 1)
     values = whole.astype(jnp.float32)
     square_mean = jnp.mean(values * values, axis=1, keepdims=True)
     normed = (values * lax.rsqrt(square_mean + 1e-06) * norm_gain[None, :, None]).astype(

time: 499 us -> 492 us (0.986)
  waiting for transfers between devices: 438 us -> 400 us
  local copies, waits for them, and re-layouts: 2.63 us -> 22.3 us
  other arithmetic: 5.68 us -> 12.1 us
    convert_element_type x0 -> x3, local copies, waits for them, and re-layouts: none -> 19.6 us  [the longest x2 18.6 us: shards(): values = whole.astype(jnp.float32)]
    all_gather x1, waiting for transfers between devices: 70.7 us -> 54 us  [shards(): lax.all_gather(w_up, 'dp', axis=0, tiled=True)]
    dot_general x0 -> x1, matrix products: none -> 11.1 us  [shards(): jnp.einsum('ukc,kf->ucf', normed, lax.all_gather(w_up, 'dp', axis=0, tile...]
    all_gather x1, waiting for transfers between devices: 80.8 us -> 70 us  [shards(): down_full = lax.all_gather(w_down, 'dp', axis=1, tiled=True)]
    all_gather x1, waiting for transfers between devices: 79.1 us -> 69.6 us  [shards(): lax.all_gather(w_gate, 'dp', axis=0, tiled=True)]
    dot_general x1, matrix products: 15.2 us -> 8.32 us  [shards(): jnp.einsum('ucf,fk->kuc', hidden, down_full, preferred_element_type=jnp.f...]
    convert_element_type x0 -> x1, other arithmetic: none -> 6.49 us  [shards(): values = whole.astype(jnp.float32)]
  transfers between devices with their start and end apart: 8 -> 8, of which waited for: 8 -> 8; matrix products, arithmetic and copies ran while one was open for 3% -> 10% of each run, Pallas kernels for 0% -> 0%
where the time goes in v1:
time: 492 us; the launch traced here: 491 us
  waiting for transfers between devices  400 us (81%)
  matrix products  42.7 us (9%)
  local copies, waits for them, and re-layouts  22.3 us (5%)
  between operations  13.5 us (3%)
  other arithmetic  12.1 us (2%)
    all_gather x1, waiting for transfers between devices, shards(): down_full = lax.all_gather(w_down, 'dp', axis=1, tiled=True)  70 us
    all_gather x1, waiting for transfers between devices, shards(): lax.all_gather(w_gate, 'dp', axis=0, tiled=True)  69.6 us
    all_gather x1, waiting for transfers between devices, shards(): lax.all_gather(w_up, 'dp', axis=0, tiled=True)  54 us
    reduce_scatter x1, waiting for transfers between devices, shards(): lax.psum_scatter(partial_value, 'mp', scatter_dimension=1, tiled=True)  50.5 us
    reduce_scatter x1, waiting for transfers between devices, shards(): lax.psum_scatter(jnp.einsum('ucf,fk->kuc', hidden, down_full, preferred_e...  49.7 us
    all_gather x1, waiting for transfers between devices, shards(): lax.all_gather(candidates, 'mp', axis=1, tiled=True)  41.3 us
    all_gather x1, waiting for transfers between devices, gathered_along(): blocks = lax.all_gather(value, mesh_axis)  34.6 us
    all_gather x1, waiting for transfers between devices, shards(): probs = lax.all_gather(probs_share, 'mp', axis=1, tiled=True)  27.9 us
  transfers between devices with their start and end apart: 8, of which 8 were waited for; matrix products, arithmetic and copies ran while one was open for 10% of the time, Pallas kernels for 0%

profile of v1, /device:TPU:0, one launch (start us, length us, event | category | flops | bytes accessed | tf_op | source)
XLA Modules:
  0.0 491.2 jit_solution(14215270502150349144)
XLA Ops:
  6.5 0.7 all-gather.8.cloned.1.call-update
  7.3 41.3 %all-gather.8.cloned.1.call-done = bf16[8,2048,128]{2,1,0:T(8,128)(2,1)} async-done(((bf16[8,256,128]{2,1,0:T(8,128)(2,1)}), bf16[8,2048,128]{2,1,0:T(8,128)(2,1)}) %all-gather.8.cloned.1.call-update) | async-done | bytes 4194320 | tf_op jit(solution)/shard_map/all_gather | solution.py:27
  48.6 8.2 %fusion.13 = f32[8,128,1024]{2,1,0:T(8,128)} fusion(bf16[8,256,1024]{2,1,0:T(8,128)(2,1)} %param.8, bf16[8,2048,128]{2,1,0:T(8,128)(2,1)} %all-gather.8.cloned.1.call-done, bf16[256,2048]{1,0:T(8,128)(2,1)S(1)} %copy-done), kind=kOutput, calls=%fused_computation.16 | convolution fusion | flops 1610874880 | bytes 13631488 | tf_op jit(solution)/shard_map/ukc,ukl->ucl/dot_general | solution.py:31
  56.8 0.6 copy-done.2
  57.5 50.5 %reduce-scatter.3.cloned.1.call-done = f32[8,16,1024]{2,1,0:T(8,128)} async-done(((f32[8,128,1024]{2,1,0:T(8,128)}), f32[8,16,1024]{2,1,0:T(8,128)}) %reduce-scatter.3.cloned.1.call-update) | async-done | bytes 524304 | tf_op jit(solution)/shard_map/reduce_scatter | solution.py:36
  108.0 1.6 fusion.25
  109.7 0.8 divide_convert_fusion
  110.6 27.9 %all-gather.10.cloned.1.call-done = bf16[8,128,1024]{2,1,0:T(8,128)(2,1)} async-done(((bf16[8,16,1024]{2,1,0:T(8,128)(2,1)}), bf16[8,128,1024]{2,1,0:T(8,128)(2,1)}) %all-gather.10.cloned.1.call-update) | async-done | bytes 2097168 | tf_op jit(solution)/shard_map/all_gather | solution.py:38
  138.4 4.4 fusion.16
  142.8 1.0 copy.11
  145.0 0.7 all-gather.16.cloned.1.call-update
  146.0 34.6 %all-gather.18.cloned.1.call-done = bf16[64,256,128]{2,1,0:T(8,128)(2,1)} async-done(((bf16[8,256,128]{2,1,0:T(8,128)(2,1)}), bf16[64,256,128]{2,1,0:T(8,128)(2,1)}) %all-gather.18.cloned.1.call-update) | async-done | bytes 4194320 | tf_op jit(solution)/shard_map/all_gather | solution.py:9
  180.6 6.5 %convert_bitcast_fusion = f32[8,8,256,128]{3,2,0,1:T(8,128)} fusion(bf16[64,256,128]{2,1,0:T(8,128)(2,1)} %all-gather.18.cloned.1.call-done), kind=kLoop, calls=%fused_computation.2 | loop fusion | flops 2097152 | bytes 12582912 | tf_op jit(solution)/shard_map/convert_element_type | solution.py:43
  187.1 9.3 %copy.12 = f32[8,8,256,128]{2,1,3,0:T(8,128)} copy(f32[8,8,256,128]{3,2,0,1:T(8,128)} %convert_bitcast_fusion) | data formatting | bytes 16777216 | tf_op jit(solution)/shard_map/convert_element_type | solution.py:43
  196.4 9.3 %reshape.33 = f32[8,2048,128]{1,2,0:T(8,128)} reshape(f32[8,8,256,128]{2,1,3,0:T(8,128)} %copy.12) | data formatting | bytes 16777216 | tf_op jit(solution)/shard_map/convert_element_type | solution.py:43
  205.7 3.0 fusion.1
  208.7 54.0 %all-gather.14.cloned.1.call-done = bf16[2048,1024]{1,0:T(8,128)(2,1)} async-done(((bf16[512,1024]{1,0:T(8,128)(2,1)}), bf16[2048,1024]{1,0:T(8,128)(2,1)}) %all-gather.14.cloned.1.call-update) | async-done | bytes 4194320 | tf_op jit(solution)/shard_map/all_gather | solution.py:57
  262.8 11.1 %fusion.4 = f32[8,128,1024]{2,1,0:T(8,128)} fusion(bf16[2048,1024]{1,0:T(8,128)(2,1)} %all-gather.14.cloned.1.call-done, f32[8,2048,128]{1,2,0:T(8,128)} %reshape.33, f32[2048]{0:T(1024)S(1)} %copy-done.3, f32[8,128]{1,0:T(8,128)S(1)} %add_rsqrt_fusion), kind=kOutput, calls=%fused_computation.7 | convolution fusion | flops 4301258752 | bytes 16789504 | tf_op jit(solution)/shard_map/ukc,kf->ucf/dot_general | solution.py:54
  273.8 69.6 %all-gather.12.cloned.1.call-done = bf16[2048,1024]{1,0:T(8,128)(2,1)} async-done(((bf16[512,1024]{1,0:T(8,128)(2,1)}), bf16[2048,1024]{1,0:T(8,128)(2,1)}) %all-gather.12.cloned.1.call-update) | async-done | bytes 4194320 | tf_op jit(solution)/shard_map/all_gather | solution.py:51
  343.4 10.8 %multiply_convert_fusion.1 = bf16[8,128,1024]{2,1,0:T(8,128)(2,1)S(1)} fusion(f32[8,128,1024]{2,1,0:T(8,128)} %fusion.4, bf16[2048,1024]{1,0:T(8,128)(2,1)} %all-gather.12.cloned.1.call-done, f32[8,2048,128]{1,2,0:T(8,128)} %reshape.33, f32[2048]{0:T(1024)S(1)} %copy-done.3, f32[8,128]{1,0:T(8,128)S(1)} %add_rsqrt_fusion), kind=kOutput, calls=%fused_computation.12 | convolution fusion | flops 4307550208 | bytes 18886656 | tf_op jit(solution)/shard_map/ukc,kf->ucf/dot_general | solution.py:48
  354.3 70.0 %all-gather.16.cloned.1.call-done = bf16[1024,2048]{1,0:T(8,128)(2,1)} async-done(((bf16[1024,512]{1,0:T(8,128)(2,1)}), bf16[1024,2048]{1,0:T(8,128)(2,1)}) %all-gather.16.cloned.1.call-update) | async-done | bytes 4194320 | tf_op jit(solution)/shard_map/all_gather | solution.py:61
  424.3 8.3 %convert_bitcast_fusion.1 = bf16[2048,8,128]{0,2,1:T(8,128)(2,1)} fusion(bf16[8,128,1024]{2,1,0:T(8,128)(2,1)S(1)} %multiply_convert_fusion.1, bf16[1024,2048]{1,0:T(8,128)(2,1)} %all-gather.16.cloned.1.call-done), kind=kOutput, calls=%fused_computation.11 | convolution fusion | flops 4297064448 | bytes 10485760 | tf_op jit(solution)/shard_map/ucf,fk->kuc/dot_general | solution.py:63
  432.6 49.7 %reduce-scatter.5.cloned.1.call-done = bf16[256,8,128]{0,2,1:T(8,128)(2,1)} async-done(((bf16[2048,8,128]{0,2,1:T(8,128)(2,1)}), bf16[256,8,128]{0,2,1:T(8,128)(2,1)}) %reduce-scatter.5.cloned.1.call-update) | async-done | bytes 524304 | tf_op jit(solution)/shard_map/reduce_scatter | solution.py:62
  482.3 2.0 copy.13
  (23 shorter events, 1.7 us)
Async XLA Ops:
  6.5 42.0 %copy-start = (bf16[256,2048]{1,0:T(8,128)(2,1)S(1)}, bf16[256,2048]{1,0:T(8,128)(2,1)}, u32[]{:S(2)}) copy-start(bf16[256,2048]{1,0:T(8,128)(2,1)} %param.11) | copy-start | bytes 3145732
  6.5 42.0 %all-gather.8.cloned.1.call-start = ((), (), s32[]{:S(2)}) async-start(), calls=%async_computation.2 | async-start | bytes 4718592 | tf_op jit(solution)/shard_map/all_gather | solution.py:27
  7.3 100.8 %reduce-scatter.3.cloned.1.call-start = ((), (), s32[]{:S(2)}) async-start(), calls=%async_computation.3 | async-start | bytes 4718592 | tf_op jit(solution)/shard_map/reduce_scatter | solution.py:36
  56.7 0.7 copy-start.2
  56.8 81.7 %all-gather.10.cloned.1.call-start = ((), (), s32[]{:S(2)}) async-start(), calls=%async_computation.4 | async-start | bytes 2359296 | tf_op jit(solution)/shard_map/all_gather | solution.py:38
  110.5 70.0 %all-gather.18.cloned.1.call-start = ((), (), s32[]{:S(2)}) async-start(), calls=%async_computation.9 | async-start | bytes 4718592 | tf_op jit(solution)/shard_map/all_gather | solution.py:9
  143.8 118.9 %all-gather.14.cloned.1.call-start = ((), (), s32[]{:S(2)}) async-start(), calls=%async_computation.6 | async-start | bytes 5242880 | tf_op jit(solution)/shard_map/all_gather | solution.py:57
  144.4 199.0 %all-gather.12.cloned.1.call-start = ((), (), s32[]{:S(2)}) async-start(), calls=%async_computation.5 | async-start | bytes 5242880 | tf_op jit(solution)/shard_map/all_gather | solution.py:51
  145.0 279.3 %all-gather.16.cloned.1.call-start = ((), (), s32[]{:S(2)}) async-start(), calls=%async_computation.7 | async-start | bytes 5242880 | tf_op jit(solution)/shard_map/all_gather | solution.py:61
  145.7 336.6 %reduce-scatter.5.cloned.1.call-start = ((), (), s32[]{:S(2)}) async-start(), calls=%async_computation.8 | async-start | bytes 4718592 | tf_op jit(solution)/shard_map/reduce_scatter | solution.py:62
  205.7 57.1 %copy-start.3 = (f32[2048]{0:T(1024)S(1)}, f32[2048]{0:T(1024)}, u32[]{:S(2)}) copy-start(f32[2048]{0:T(1024)} %param.12) | copy-start | bytes 24580
  424.3 60.1 %copy-start.1 = (bf16[256,2048]{1,0:T(8,128)(2,1)S(1)}, bf16[256,2048]{1,0:T(8,128)(2,1)}, u32[]{:S(2)}) copy-start(bf16[256,2048]{1,0:T(8,128)(2,1)} %param.11) | copy-start | bytes 3145732
Sparse Core Ops, SparseCore 0:
  9.2 39.2 all-gather.7
  56.9 51.0 reduce-scatter.2
  110.6 27.7 all-gather.9
  144.0 36.5 all-gather.17
  182.0 80.7 all-gather.13
  264.2 79.2 all-gather.11
  345.0 79.2 all-gather.15
  432.7 49.5 reduce-scatter.4
